TPU v7x, 32 devices: a whole 2x2x4 slice. The times are simulated.
32 devices in a mesh: group: 2 (over x), dom: 16 (over z, y, core).
Axes of the slice: x: 2, y: 2, z: 4, core: 2. Of those that a mesh axis runs over, the one named last changes fastest.
Arguments:
- features: bfloat16 [8192, 512], P(('group', 'dom')), may hold values from -6 to 6
- tile_columns: int32 [32, 2, 4], P(('group', 'dom')), may hold values from 0 to 1
- tile_values: bfloat16 [32, 2, 4, 128, 128], P(('group', 'dom')), as said below
- send_rows: int32 [32, 16, 16], P(('group', 'dom')), may hold values from 0 to 255
- send_count: int32 [32, 16], P(('group', 'dom')), may hold values from 0 to 16, as said below
- ghost_target: int32 [32, 16, 16], P(('group', 'dom')), may hold values from 0 to 255
- query_rows: int32 [32, 512], P(('group', 'dom')), may hold values from 0 to 255
- positive_cand: int32 [32, 512], P(('group', 'dom')), may hold values from 0 to 63
- negative_rows: int32 [32, 32], P(('group', 'dom')), may hold values from 0 to 255
- weight_self: bfloat16 [512, 512], replicated, may hold values from -0.25 to 0.25
- weight_neigh: bfloat16 [512, 512], replicated, may hold values from -0.75 to 0.75
Outputs:
- embeddings: bfloat16 [8192, 512], P(('group', 'dom'))
- weight_grads: bfloat16 [1024, 512], P('dom')
Inputs may be any that keep to these rules, and one draw needn't show every extreme that they name: `send_count`: no device sends rows to its own index of dom; in every group one index of dom receives exactly 16 rows from every other index. `tile_values`: weights are zero or between 0.5 and 1.
All inputs are finite; a program needn't handle non-finite values.
Results may differ from a plain program's by a relative error of at most 0.015.
Values may be sent and summed in bfloat16 or wider, within the bound.
No kernel may reach another device: no remote copies, remote signals or barrier semaphores. Data moves between devices by JAX's collectives and lax.ppermute only.
A program may use at most 64 MiB of HBM per device.

v0:
```python
import math
import jax
import jax.numpy as jnp
from jax import lax
from jax.sharding import PartitionSpec as P

LOSS_FACTOR = 64.0
EPSILON = 1e-05


def score_grads(scores, positive, cand_total, query_total):
    sigma = jax.nn.sigmoid(scores)
    dscore = jnp.where(positive, sigma - 1.0, sigma / (cand_total - 1.0)) * (
        LOSS_FACTOR / query_total
    )
    return dscore.astype(jnp.bfloat16)


def transpose_dot(left, right):
    return lax.dot_general(
        left, right, (((0,), (0,)), ((), ())), preferred_element_type=jnp.float32
    )


def on_device(
    features,
    tile_columns,
    tile_values,
    send_rows,
    send_count,
    ghost_target,
    query_rows,
    positive_cand,
    negative_rows,
    weight_self,
    weight_neigh,
):
    node_count, width = features.shape
    row_blocks, tiles_row, tile_size = (
        tile_values.shape[1],
        tile_values.shape[2],
        tile_values.shape[3],
    )
    slot_count = send_rows.shape[2]
    group_count = lax.axis_size("group")
    score_factor = 1.0 / math.sqrt(width)
    outgoing = features[send_rows[0]]
    flags = (jnp.arange(slot_count, dtype=jnp.int32)[None, :] < send_count[0][:, None]).astype(
        jnp.bfloat16
    )
    received, flags_in = (
        lax.all_to_all(outgoing, "dom", split_axis=0, concat_axis=0, tiled=True),
        lax.all_to_all(flags, "dom", split_axis=0, concat_axis=0, tiled=True),
    )
    blocks = features.reshape(row_blocks, tile_size, width)
    picked = blocks[tile_columns[0]]
    local = jnp.einsum(
        "rtij,rtjd->rid", tile_values[0], picked, preferred_element_type=jnp.float32
    ).reshape(node_count, width)
    row_weight = jnp.sum(tile_values[0].astype(jnp.float32), axis=(1, 3)).reshape(node_count)
    live = flags_in.astype(jnp.float32)
    targets = ghost_target[0].reshape(-1)
    weighted = (received.astype(jnp.float32) * live[:, :, None]).reshape(-1, width)
    ghost_sum = jnp.zeros((node_count, width), jnp.float32).at[targets].add(weighted)
    ghost_count = jnp.zeros((node_count,), jnp.float32).at[targets].add(live.reshape(-1))
    degree = 1.0 + row_weight + ghost_count
    aggregate = ((local + ghost_sum) / degree[:, None]).astype(jnp.bfloat16)
    pre = jnp.dot(features, weight_self, preferred_element_type=jnp.float32) + jnp.dot(
        aggregate, weight_neigh, preferred_element_type=jnp.float32
    )
    scale = lax.rsqrt(jnp.mean(pre * pre, axis=-1, keepdims=True) + EPSILON)
    embeds = (pre * scale).astype(jnp.bfloat16)
    queries = embeds[query_rows[0]]
    own_negs = embeds[negative_rows[0]]
    neg_count = own_negs.shape[0]
    query_total = queries.shape[0]
    cand_total = neg_count * group_count
    targets_pos = positive_cand[0][:, None]
    all_negs = lax.all_gather(own_negs, "group", axis=0, tiled=True)
    scores = score_factor * jnp.dot(queries, all_negs.T, preferred_element_type=jnp.float32)
    positive = targets_pos == jnp.arange(cand_total, dtype=jnp.int32)[None, :]
    dscore = score_grads(scores, positive, cand_total, query_total)
    query_grad = score_factor * jnp.dot(dscore, all_negs, preferred_element_type=jnp.float32)
    neg_grad = lax.psum_scatter(
        (score_factor * transpose_dot(dscore, queries)).astype(jnp.bfloat16),
        "group",
        scatter_dimension=0,
        tiled=True,
    ).astype(jnp.float32)
    emb_grad = jnp.zeros((node_count, width), jnp.float32)
    emb_grad = emb_grad.at[query_rows[0]].add(query_grad)
    emb_grad = emb_grad.at[negative_rows[0]].add(neg_grad)
    inner = jnp.mean(pre * emb_grad, axis=-1, keepdims=True)
    pre_grad = (scale * emb_grad - pre * scale * scale * scale * inner).astype(jnp.bfloat16)
    stacked = jnp.concatenate([features, aggregate], axis=1)
    shard = lax.psum_scatter(
        transpose_dot(stacked, pre_grad), "dom", scatter_dimension=0, tiled=True
    )
    summed = lax.psum(shard.astype(jnp.bfloat16), "group")
    return (embeds, summed)


def solution(mesh):
    placed = (
        P(("group", "dom"), None),
        P(("group", "dom"), None, None),
        P(("group", "dom"), None, None, None, None),
        P(("group", "dom"), None, None),
        P(("group", "dom"), None),
        P(("group", "dom"), None, None),
        P(("group", "dom"), None),
        P(("group", "dom"), None),
        P(("group", "dom"), None),
        P(),
        P(),
    )
    return jax.shard_map(
        on_device,
        mesh=mesh,
        in_specs=placed,
        out_specs=(P(("group", "dom"), None), P("dom", None)),
        check_vma=False,
    )
```

profile of v0, /device:TPU:0, one launch (start us, length us, event | category | flops | bytes accessed | tf_op | source)
XLA Modules:
  0.0 157.0 jit_solution(12821754926774188139)
XLA Ops:
  7.2 1.4 compare_convert_fusion
  8.6 7.4 %all-to-all-start.1 = ((bf16[16,1,16]{2,1,0:T(2,128)(2,1)}), bf16[16,1,16]{2,1,0:T(2,128)(2,1)S(1)}, u32[]{:S(2)}, u32[]{:S(2)}) async-start(bf16[16,1,16]{2,1,0:T(2,128)(2,1)} %compare_convert_fusion), calls=%async_computation.1 | async-start | bytes 16384 | tf_op jit(solution)/shard_map/all_to_all | solution.py:53
  16.7 0.7 compare_select_fusion.3
  17.4 0.8 reshape_squeeze.3
  18.2 1.1 convert_reduce_fusion
  19.3 0.7 compare_select_fusion.1
  20.0 0.7 compare_select_fusion
  20.8 1.4 fusion.19
  22.3 1.9 %gather_fusion.1 = bf16[256,512]{1,0:T(8,128)(2,1)} fusion(bf16[256,512]{1,0:T(8,128)(2,1)S(1)} %copy-done.2, s32[1024]{0:T(1024)S(1)} %pad_clamp_fusion.2), kind=kCustom, calls=%fused_computation.1 | custom fusion | bytes 525312 | tf_op jit(solution)/shard_map/gather | solution.py:47
  24.8 6.0 %all-to-all-start = ((bf16[16,16,512]{2,1,0:T(8,128)(2,1)}), bf16[16,16,512]{2,1,0:T(8,128)(2,1)S(1)}, u32[]{:S(2)}, u32[]{:S(2)}) async-start(bf16[16,16,512]{2,1,0:T(8,128)(2,1)} %bitcast.10), calls=%async_computation | async-start | bytes 524288 | tf_op jit(solution)/shard_map/all_to_all | solution.py:52
  31.3 2.3 %scatter_fusion.1 = f32[256]{0:T(256)S(1)} fusion(f32[256]{0:T(256)S(1)} %add_bitcast_fusion, s32[256]{0:T(256)S(1)} %bitcast.51, f32[256]{0:T(256)S(1)} %reshape.273), kind=kCustom, calls=%fused_computation.5 | custom fusion | flops 256 | bytes 4096 | tf_op jit(solution)/shard_map/scatter-add | solution.py:65
  33.6 7.2 %all-to-all-done = bf16[16,16,512]{2,1,0:T(8,128)(2,1)S(1)} async-done(((bf16[16,16,512]{2,1,0:T(8,128)(2,1)}), bf16[16,16,512]{2,1,0:T(8,128)(2,1)S(1)}, u32[]{:S(2)}, u32[]{:S(2)}) %all-to-all-start) | async-done | bytes 262176 | tf_op jit(solution)/shard_map/all_to_all | solution.py:52
  40.9 2.3 %scatter_fusion = f32[256,512]{1,0:T(8,128)S(1)} fusion(f32[256,512]{1,0:T(8,128)S(1)} %bitcast.46, s32[256]{0:T(256)S(1)} %bitcast.52, f32[256,512]{1,0:T(8,128)S(1)} %bitcast.49), kind=kCustom, calls=%fused_computation.4 | custom fusion | flops 131072 | bytes 1573888 | tf_op jit(solution)/shard_map/scatter-add | solution.py:64
  44.5 4.6 %all-gather = bf16[64,512]{1,0:T(8,128)(2,1)S(1)} all-gather(bf16[32,512]{1,0:T(8,128)(2,1)S(1)} %gather_fusion.3), channel_id=2, replica_groups=mesh['group'=2,'dom'=16] {'group'}, dimensions={0}, use_global_device_ids=true | all-gather | bytes 98304 | tf_op jit(solution)/shard_map/all_gather | solution.py:79
  49.1 2.0 %gather_fusion.2 = bf16[512,512]{1,0:T(8,128)(2,1)S(1)} fusion(bf16[256,512]{1,0:T(8,128)(2,1)S(1)} %multiply_convert_fusion, s32[1024]{0:T(1024)S(1)} %pad_clamp_fusion.1), kind=kCustom, calls=%fused_computation.2 | custom fusion | bytes 1050624 | tf_op jit(solution)/shard_map/gather | solution.py:73
  51.4 0.8 fusion.4
  52.6 3.7 %scatter_custom_fusion.2 = f32[256,512]{1,0:T(8,128)S(1)} fusion(s32[512]{0:T(512)S(1)} %bitcast.54, f32[512,512]{1,0:T(8,128)S(1)} %convolution_multiply_fusion, f32[]{:T(128)} %constant.14.clone.1), kind=kCustom, calls=%fused_computation.31 | custom fusion | flops 262144 | bytes 524292 | tf_op jit(solution)/shard_map/scatter-add | solution.py:91
  56.4 4.3 %reduce-scatter.3.cloned.1.call-done = bf16[32,512]{1,0:T(8,128)(2,1)} async-done(((bf16[64,512]{1,0:T(8,128)(2,1)}), bf16[32,512]{1,0:T(8,128)(2,1)}) %reduce-scatter.3.cloned.1.call-update) | async-done | bytes 32784 | tf_op jit(solution)/shard_map/reduce_scatter | solution.py:84
  60.6 1.2 scatter_custom_fusion.3
  62.0 2.0 %fusion.5 = f32[1024,512]{1,0:T(8,128)} fusion(bf16[256,512]{1,0:T(8,128)(2,1)S(1)} %divide_convert_fusion, bf16[256,512]{1,0:T(8,128)(2,1)S(1)} %copy-done.2, f32[256,512]{1,0:T(8,128)S(1)} %scatter_custom_fusion.3, f32[256,512]{1,0:T(8,128)S(1)} %get-tuple-element.3, f32[256]{0:T(256)S(1)} %broadcast_multiply_fusion, f32[256]{0:T(256)S(1)} %add_rsqrt_fusion), kind=kOutput, calls=%fused_computation.17 | convolution fusion | flops 270401536 | bytes 3672064 | tf_op jit(solution)/shard_map/dot_general | solution.py:20
  64.0 62.2 %reduce-scatter.5.cloned.1.call-done = f32[64,512]{1,0:T(8,128)} async-done(((f32[1024,512]{1,0:T(8,128)}), f32[64,512]{1,0:T(8,128)}) %reduce-scatter.5.cloned.1.call-update) | async-done | bytes 131088 | tf_op jit(solution)/shard_map/reduce_scatter | solution.py:96
  126.2 1.5 convert_element_type.66
  127.8 21.2 %all-reduce.2.cloned.1.call-done = bf16[64,512]{1,0:T(8,128)(2,1)} async-done(((bf16[64,512]{1,0:T(8,128)(2,1)}), bf16[64,512]{1,0:T(8,128)(2,1)}) %all-reduce.2.cloned.1.call-update) | async-done | bytes 65552 | tf_op jit(solution)/shard_map/psum | solution.py:99
  149.0 1.5 copy.18
  (41 shorter events, 4.2 us)
Async XLA Ops:
  7.2 36.2 %copy-start = (bf16[512,512]{1,0:T(8,128)(2,1)S(1)}, bf16[512,512]{1,0:T(8,128)(2,1)}, u32[]{:S(2)}) copy-start(bf16[512,512]{1,0:T(8,128)(2,1)} %param.21) | copy-start | bytes 1572868
  7.2 15.1 %copy-start.2 = (bf16[256,512]{1,0:T(8,128)(2,1)S(1)}, bf16[256,512]{1,0:T(8,128)(2,1)}, u32[]{:S(2)}) copy-start(bf16[256,512]{1,0:T(8,128)(2,1)} %param.11) | copy-start | bytes 786436
  8.6 16.1 %all-to-all-start.1 = ((bf16[16,1,16]{2,1,0:T(2,128)(2,1)}), bf16[16,1,16]{2,1,0:T(2,128)(2,1)S(1)}, u32[]{:S(2)}, u32[]{:S(2)}) async-start(bf16[16,1,16]{2,1,0:T(2,128)(2,1)} %compare_convert_fusion), calls=%async_computation.1 | async-start | bytes 16384 | tf_op jit(solution)/shard_map/all_to_all | solution.py:53
  22.3 8.6 %copy-start.3 = (bf16[1,2,4,128,128]{4,3,2,1,0:T(8,128)(2,1)S(1)}, bf16[1,2,4,128,128]{4,3,2,1,0:T(8,128)(2,1)}, u32[]{:S(2)}) copy-start(bf16[1,2,4,128,128]{4,3,2,1,0:T(8,128)(2,1)} %param.13) | copy-start | bytes 786436
  24.8 16.0 %all-to-all-start = ((bf16[16,16,512]{2,1,0:T(8,128)(2,1)}), bf16[16,16,512]{2,1,0:T(8,128)(2,1)S(1)}, u32[]{:S(2)}, u32[]{:S(2)}) async-start(bf16[16,16,512]{2,1,0:T(8,128)(2,1)} %bitcast.10), calls=%async_computation | async-start | bytes 524288 | tf_op jit(solution)/shard_map/all_to_all | solution.py:52
  30.8 29.9 %reduce-scatter.3.cloned.1.call-start = ((), (), s32[]{:S(2)}) async-start(), calls=%async_computation.4 | async-start | bytes 98304 | tf_op jit(solution)/shard_map/reduce_scatter | solution.py:84
  43.9 7.2 %copy-start.1 = (bf16[256,512]{1,0:T(8,128)(2,1)}, bf16[256,512]{1,0:T(8,128)(2,1)S(1)}, u32[]{:S(2)}) copy-start(bf16[256,512]{1,0:T(8,128)(2,1)S(1)} %multiply_convert_fusion) | copy-start | bytes 786436
  49.1 2.0 %copy-start.4 = (s32[1,512]{1,0:T(1,128)S(1)}, s32[1,512]{1,0:T(1,128)}, u32[]{:S(2)}) copy-start(s32[1,512]{1,0:T(1,128)} %param.18) | copy-start | bytes 6148
  52.3 74.0 %reduce-scatter.5.cloned.1.call-start = ((), (), s32[]{:S(2)}) async-start(), calls=%async_computation.5 | async-start | bytes 2228224 | tf_op jit(solution)/shard_map/reduce_scatter | solution.py:96
  64.0 85.0 %all-reduce.2.cloned.1.call-start = ((), (), s32[]{:S(2)}) async-start(), calls=%async_computation.6 | async-start | bytes 131072 | tf_op jit(solution)/shard_map/psum | solution.py:99
Sparse Core Ops, SparseCore 0:
  52.4 8.1 reduce-scatter.2
  64.4 61.8 reduce-scatter.4
  129.1 19.8 all-reduce.1
where the time goes:
time: 158 us; the launch traced here: 157 us
  waiting for transfers between devices  94.9 us (60%)
  other arithmetic  16.8 us (11%)
  between operations  14 us (9%)
  starting transfers between devices  13.6 us (9%)
  local copies, waits for them, and re-layouts  7.58 us (5%)
  matrix products  5.54 us (4%)
  blocking collectives  4.58 us (3%)
    reduce_scatter x1, waiting for transfers between devices, on_device(): lax.psum_scatter(transpose_dot(stacked, pre_grad), 'dom', scatter_dimensi...  62.2 us
    psum x1, waiting for transfers between devices, on_device(): summed = lax.psum(shard.astype(jnp.bfloat16), 'group')  21.2 us
    all_to_all x1, starting transfers between devices, on_device(): lax.all_to_all(flags, 'dom', split_axis=0, concat_axis=0, tiled=True)  7.41 us
    all_to_all x1, waiting for transfers between devices, on_device(): lax.all_to_all(outgoing, 'dom', split_axis=0, concat_axis=0, tiled=True)  7.18 us
    all_to_all x1, starting transfers between devices, on_device(): lax.all_to_all(outgoing, 'dom', split_axis=0, concat_axis=0, tiled=True)  6.02 us
    all_gather x1, blocking collectives, on_device(): all_negs = lax.all_gather(own_negs, 'group', axis=0, tiled=True)  4.58 us
    reduce_scatter x1, waiting for transfers between devices, on_device(): lax.psum_scatter((score_factor * transpose_dot(dscore, queries)).astype(j...  4.28 us
    scatter-add x1, other arithmetic, on_device(): emb_grad = emb_grad.at[query_rows[0]].add(query_grad)  3.71 us
  transfers between devices with their start and end apart: 5, of which 4 were waited for; matrix products, arithmetic and copies ran while one was open for 10% of the time, Pallas kernels for 0%

commit v1 on v0

--- a/solution.py
+++ b/solution.py
@@ -3,9 +3,29 @@
 import jax.numpy as jnp
 from jax import lax
 from jax.sharding import PartitionSpec as P
+from jax.lax import axis_index, axis_size, ppermute
 
 LOSS_FACTOR = 64.0
 EPSILON = 1e-05
+
+
+def lots_all_pack(content):
+    current_value = axis_index("dom")
+    part_now = axis_size("dom")
+    field_out, z_new = (part_now, current_value)
+    carry = list(content.shape)
+    block_now = content.shape[0] // field_out
+    carry[0] = block_now
+    mat_out = carry[0]
+    carry[0] = mat_out * field_out
+    small = jnp.zeros(carry, content.dtype)
+    for u in range(field_out):
+        latest = lax.dynamic_slice_in_dim(content, (z_new ^ u) * block_now, block_now, axis=0)
+        if u:
+            kept_arr = list(map(lambda i: (i, i ^ u), range(field_out)))
+            latest = ppermute(latest, axis_name="dom", perm=kept_arr)
+        small = lax.dynamic_update_slice_in_dim(small, latest, (z_new ^ u) * mat_out, axis=0)
+    return small
 
 
 def score_grads(scores, positive, cand_total, query_total):
@@ -49,7 +69,7 @@
         jnp.bfloat16
     )
     received, flags_in = (
-        lax.all_to_all(outgoing, "dom", split_axis=0, concat_axis=0, tiled=True),
+        lots_all_pack(outgoing),
         lax.all_to_all(flags, "dom", split_axis=0, concat_axis=0, tiled=True),
     )
     blocks = features.reshape(row_blocks, tile_size, width)

time: 158 us -> 201 us (1.27)
  waiting for transfers between devices: 94.9 us -> 123 us
  starting transfers between devices: 13.6 us -> 25.2 us
  local copies, waits for them, and re-layouts: 7.58 us -> 11.7 us
    ppermute x0 -> x15, waiting for transfers between devices: none -> 33 us  [lots_all_pack(): latest = ppermute(latest, axis_name='dom', perm=kept_arr)]
    ppermute x0 -> x15, starting transfers between devices: none -> 17.7 us  [lots_all_pack(): latest = ppermute(latest, axis_name='dom', perm=kept_arr)]
    all_to_all x1 -> x0, waiting for transfers between devices: 7.18 us -> none  [on_device(): lax.all_to_all(outgoing, 'dom', split_axis=0, concat_axis=0, tiled=True)]
    all_to_all x1 -> x0, starting transfers between devices: 6.02 us -> none  [on_device(): lax.all_to_all(outgoing, 'dom', split_axis=0, concat_axis=0, tiled=True)]
    dynamic_update_slice x0 -> x15, local copies, waits for them, and re-layouts: none -> 3.63 us  [lots_all_pack(): lax.dynamic_update_slice_in_dim(small, latest, (z_new ^ u) * mat_out, axi...]
    reduce_scatter x1, waiting for transfers between devices: 4.28 us -> 6.99 us  [on_device(): lax.psum_scatter((score_factor * transpose_dot(dscore, queries)).astype(j...]
  transfers between devices with their start and end apart: 5 -> 19, of which waited for: 4 -> 13; matrix products, arithmetic and copies ran while one was open for 10% -> 9% of each run, Pallas kernels for 0% -> 0%
where the time goes in v1:
time: 201 us; the launch traced here: 200 us
  waiting for transfers between devices  123 us (61%)
  starting transfers between devices  25.2 us (13%)
  other arithmetic  16.4 us (8%)
  between operations  14.2 us (7%)
  local copies, waits for them, and re-layouts  11.7 us (6%)
  blocking collectives  4.58 us (2%)
  matrix products  4.4 us (2%)
    reduce_scatter x1, waiting for transfers between devices, on_device(): lax.psum_scatter(transpose_dot(stacked, pre_grad), 'dom', scatter_dimensi...  62.2 us
    ppermute x15, waiting for transfers between devices, lots_all_pack(): latest = ppermute(latest, axis_name='dom', perm=kept_arr)  33 us
    psum x1, waiting for transfers between devices, on_device(): summed = lax.psum(shard.astype(jnp.bfloat16), 'group')  21.1 us
    ppermute x15, starting transfers between devices, lots_all_pack(): latest = ppermute(latest, axis_name='dom', perm=kept_arr)  17.7 us
    all_to_all x1, starting transfers between devices, on_device(): lax.all_to_all(flags, 'dom', split_axis=0, concat_axis=0, tiled=True)  7.41 us
    reduce_scatter x1, waiting for transfers between devices, on_device(): lax.psum_scatter((score_factor * transpose_dot(dscore, queries)).astype(j...  6.99 us
    all_gather x1, blocking collectives, on_device(): all_negs = lax.all_gather(own_negs, 'group', axis=0, tiled=True)  4.58 us
  transfers between devices with their start and end apart: 19, of which 13 were waited for; matrix products, arithmetic and copies ran while one was open for 9% of the time, Pallas kernels for 0%

profile of v1, /device:TPU:0, one launch (start us, length us, event | category | flops | bytes accessed | tf_op | source)
XLA Modules:
  0.0 199.9 jit_solution(1056349425236211260)
XLA Ops:
  8.7 7.4 %all-to-all-start = ((bf16[16,1,16]{2,1,0:T(2,128)(2,1)}), bf16[16,1,16]{2,1,0:T(2,128)(2,1)S(1)}, u32[]{:S(2)}, u32[]{:S(2)}) async-start(bf16[16,1,16]{2,1,0:T(2,128)(2,1)} %compare_convert_fusion), calls=%async_computation | async-start | bytes 16384 | tf_op jit(solution)/shard_map/all_to_all | solution.py:73
  17.1 2.2 %gather_fusion.1 = bf16[256,512]{1,0:T(8,128)(2,1)S(1)} fusion(bf16[256,512]{1,0:T(8,128)(2,1)} %param.11, s32[1024]{0:T(1024)S(1)} %pad_clamp_fusion.2), kind=kCustom, calls=%fused_computation.1 | custom fusion | bytes 525312 | tf_op jit(solution)/shard_map/gather | solution.py:67
  20.1 4.3 %collective-permute-start.14 = (bf16[1,16,512]{2,1,0:T(8,128)(2,1)S(1)}, bf16[1,16,512]{2,1,0:T(8,128)(2,1)}, u32[]{:S(2)}, u32[]{:S(2)}) collective-permute-start(bf16[1,16,512]{2,1,0:T(8,128)(2,1)S(1)} %get-tuple-element.2), channel_id=1, source_target_pairs={{0,15},{1,14},{2,13},{3,12},{4,11},{5,10},{6,9},{7,8},{8,7},{9,6},... | collective-permute-start | bytes 49160 | tf_op jit(solution)/shard_map/ppermute | solution.py:26
  24.8 3.2 %collective-permute-start.12 = (bf16[1,16,512]{2,1,0:T(8,128)(2,1)S(1)}, bf16[1,16,512]{2,1,0:T(8,128)(2,1)}, u32[]{:S(2)}, u32[]{:S(2)}) collective-permute-start(bf16[1,16,512]{2,1,0:T(8,128)(2,1)S(1)} %get-tuple-element.4), channel_id=1, source_target_pairs={{0,13},{1,12},{2,15},{3,14},{4,9},{5,8},{6,11},{7,10},{8,5},{9,4},... | collective-permute-start | bytes 49160 | tf_op jit(solution)/shard_map/ppermute | solution.py:26
  32.6 2.3 %scatter_fusion.1 = f32[256]{0:T(256)S(1)} fusion(f32[256]{0:T(256)S(1)} %add_bitcast_fusion, s32[256]{0:T(256)S(1)} %bitcast.52, f32[256]{0:T(256)S(1)} %reshape.273), kind=kCustom, calls=%fused_computation.5 | custom fusion | flops 256 | bytes 4096 | tf_op jit(solution)/shard_map/scatter-add | solution.py:85
  39.5 2.9 %collective-permute-done.2 = bf16[1,16,512]{2,1,0:T(8,128)(2,1)S(1)} collective-permute-done((bf16[1,16,512]{2,1,0:T(8,128)(2,1)}, bf16[1,16,512]{2,1,0:T(8,128)(2,1)S(1)}, u32[]{:S(2)}, u32[]{:S(2)}) %collective-permute-start.2) | collective-permute-done | bytes 16416 | tf_op jit(solution)/shard_map/ppermute | solution.py:26
  42.4 3.9 %collective-permute-done.3 = bf16[1,16,512]{2,1,0:T(8,128)(2,1)S(1)} collective-permute-done((bf16[1,16,512]{2,1,0:T(8,128)(2,1)}, bf16[1,16,512]{2,1,0:T(8,128)(2,1)S(1)}, u32[]{:S(2)}, u32[]{:S(2)}) %collective-permute-start.3) | collective-permute-done | bytes 16416 | tf_op jit(solution)/shard_map/ppermute | solution.py:26
  46.3 3.4 %collective-permute-done.4 = bf16[1,16,512]{2,1,0:T(8,128)(2,1)S(1)} collective-permute-done((bf16[1,16,512]{2,1,0:T(8,128)(2,1)}, bf16[1,16,512]{2,1,0:T(8,128)(2,1)S(1)}, u32[]{:S(2)}, u32[]{:S(2)}) %collective-permute-start.4) | collective-permute-done | bytes 16416 | tf_op jit(solution)/shard_map/ppermute | solution.py:26
  50.8 3.8 %collective-permute-done.5 = bf16[1,16,512]{2,1,0:T(8,128)(2,1)S(1)} collective-permute-done((bf16[1,16,512]{2,1,0:T(8,128)(2,1)}, bf16[1,16,512]{2,1,0:T(8,128)(2,1)S(1)}, u32[]{:S(2)}, u32[]{:S(2)}) %collective-permute-start.5) | collective-permute-done | bytes 16416 | tf_op jit(solution)/shard_map/ppermute | solution.py:26
  54.5 4.3 %collective-permute-done.6 = bf16[1,16,512]{2,1,0:T(8,128)(2,1)S(1)} collective-permute-done((bf16[1,16,512]{2,1,0:T(8,128)(2,1)}, bf16[1,16,512]{2,1,0:T(8,128)(2,1)S(1)}, u32[]{:S(2)}, u32[]{:S(2)}) %collective-permute-start.6) | collective-permute-done | bytes 16416 | tf_op jit(solution)/shard_map/ppermute | solution.py:26
  58.8 2.1 %collective-permute-start.7 = (bf16[1,16,512]{2,1,0:T(8,128)(2,1)S(1)}, bf16[1,16,512]{2,1,0:T(8,128)(2,1)S(1)}, u32[]{:S(2)}, u32[]{:S(2)}) collective-permute-start(bf16[1,16,512]{2,1,0:T(8,128)(2,1)S(1)} %get-tuple-element.9), channel_id=1, source_target_pairs={{0,8},{1,9},{2,10},{3,11},{4,12},{5,13},{6,14},{7,15},{8,0},{9,1},... | collective-permute-start | bytes 49160 | tf_op jit(solution)/shard_map/ppermute | solution.py:26
  61.0 2.5 %collective-permute-done.7 = bf16[1,16,512]{2,1,0:T(8,128)(2,1)S(1)} collective-permute-done((bf16[1,16,512]{2,1,0:T(8,128)(2,1)S(1)}, bf16[1,16,512]{2,1,0:T(8,128)(2,1)S(1)}, u32[]{:S(2)}, u32[]{:S(2)}) %collective-permute-start.7) | collective-permute-done | bytes 16416 | tf_op jit(solution)/shard_map/ppermute | solution.py:26
  64.3 3.2 %collective-permute-done.8 = bf16[1,16,512]{2,1,0:T(8,128)(2,1)S(1)} collective-permute-done((bf16[1,16,512]{2,1,0:T(8,128)(2,1)S(1)}, bf16[1,16,512]{2,1,0:T(8,128)(2,1)S(1)}, u32[]{:S(2)}, u32[]{:S(2)}) %collective-permute-start.8) | collective-permute-done | bytes 16416 | tf_op jit(solution)/shard_map/ppermute | solution.py:26
  67.5 2.9 %collective-permute-start.9 = (bf16[1,16,512]{2,1,0:T(8,128)(2,1)S(1)}, bf16[1,16,512]{2,1,0:T(8,128)(2,1)S(1)}, u32[]{:S(2)}, u32[]{:S(2)}) collective-permute-start(bf16[1,16,512]{2,1,0:T(8,128)(2,1)S(1)} %get-tuple-element.7), channel_id=1, source_target_pairs={{0,10},{1,11},{2,8},{3,9},{4,14},{5,15},{6,12},{7,13},{8,2},{9,3},... | collective-permute-start | bytes 49160 | tf_op jit(solution)/shard_map/ppermute | solution.py:26
  70.4 2.7 %collective-permute-done.9 = bf16[1,16,512]{2,1,0:T(8,128)(2,1)S(1)} collective-permute-done((bf16[1,16,512]{2,1,0:T(8,128)(2,1)S(1)}, bf16[1,16,512]{2,1,0:T(8,128)(2,1)S(1)}, u32[]{:S(2)}, u32[]{:S(2)}) %collective-permute-start.9) | collective-permute-done | bytes 16416 | tf_op jit(solution)/shard_map/ppermute | solution.py:26
  73.2 4.8 %collective-permute-done.10 = bf16[1,16,512]{2,1,0:T(8,128)(2,1)S(1)} collective-permute-done((bf16[1,16,512]{2,1,0:T(8,128)(2,1)S(1)}, bf16[1,16,512]{2,1,0:T(8,128)(2,1)S(1)}, u32[]{:S(2)}, u32[]{:S(2)}) %collective-permute-start.10) | collective-permute-done | bytes 16416 | tf_op jit(solution)/shard_map/ppermute | solution.py:26
  81.0 2.3 %scatter_fusion = f32[256,512]{1,0:T(8,128)S(1)} fusion(f32[256,512]{1,0:T(8,128)S(1)} %bitcast.46, s32[256]{0:T(256)S(1)} %bitcast.53, f32[256,512]{1,0:T(8,128)S(1)} %bitcast.49), kind=kCustom, calls=%fused_computation.4 | custom fusion | flops 131072 | bytes 1573888 | tf_op jit(solution)/shard_map/scatter-add | solution.py:84
  84.6 4.6 %all-gather = bf16[64,512]{1,0:T(8,128)(2,1)S(1)} all-gather(bf16[32,512]{1,0:T(8,128)(2,1)S(1)} %gather_fusion.3), channel_id=2, replica_groups=mesh['group'=2,'dom'=16] {'group'}, dimensions={0}, use_global_device_ids=true | all-gather | bytes 98304 | tf_op jit(solution)/shard_map/all_gather | solution.py:99
  89.2 2.0 gather_fusion.2
  92.8 3.8 %scatter_custom_fusion.2 = f32[256,512]{1,0:T(8,128)S(1)} fusion(s32[512]{0:T(512)} %bitcast.55, f32[512,512]{1,0:T(8,128)S(1)} %convolution_multiply_fusion, f32[]{:T(128)} %constant.11.clone.1), kind=kCustom, calls=%fused_computation.31 | custom fusion | flops 262144 | bytes 524800 | tf_op jit(solution)/shard_map/scatter-add | solution.py:111
  96.6 7.0 %reduce-scatter.3.cloned.1.call-done = bf16[32,512]{1,0:T(8,128)(2,1)} async-done(((bf16[64,512]{1,0:T(8,128)(2,1)}), bf16[32,512]{1,0:T(8,128)(2,1)}) %reduce-scatter.3.cloned.1.call-update) | async-done | bytes 32784 | tf_op jit(solution)/shard_map/reduce_scatter | solution.py:104
  105.0 1.9 fusion.5
  107.0 62.2 %reduce-scatter.5.cloned.1.call-done = f32[64,512]{1,0:T(8,128)} async-done(((f32[1024,512]{1,0:T(8,128)}), f32[64,512]{1,0:T(8,128)}) %reduce-scatter.5.cloned.1.call-update) | async-done | bytes 131088 | tf_op jit(solution)/shard_map/reduce_scatter | solution.py:116
  170.7 21.1 %all-reduce.2.cloned.1.call-done = bf16[64,512]{1,0:T(8,128)(2,1)} async-done(((bf16[64,512]{1,0:T(8,128)(2,1)}), bf16[64,512]{1,0:T(8,128)(2,1)}) %all-reduce.2.cloned.1.call-update) | async-done | bytes 65552 | tf_op jit(solution)/shard_map/psum | solution.py:119
  (100 shorter events, 24.8 us)
Async XLA Ops:
  7.2 76.3 %copy-start = (bf16[512,512]{1,0:T(8,128)(2,1)S(1)}, bf16[512,512]{1,0:T(8,128)(2,1)}, u32[]{:S(2)}) copy-start(bf16[512,512]{1,0:T(8,128)(2,1)} %param.21) | copy-start | bytes 1572868
  7.2 23.3 %copy-start.2 = (bf16[256,512]{1,0:T(8,128)(2,1)S(1)}, bf16[256,512]{1,0:T(8,128)(2,1)}, u32[]{:S(2)}) copy-start(bf16[256,512]{1,0:T(8,128)(2,1)} %param.11) | copy-start | bytes 786436
  7.2 21.9 %copy-start.3 = (bf16[1,2,4,128,128]{4,3,2,1,0:T(8,128)(2,1)S(1)}, bf16[1,2,4,128,128]{4,3,2,1,0:T(8,128)(2,1)}, u32[]{:S(2)}) copy-start(bf16[1,2,4,128,128]{4,3,2,1,0:T(8,128)(2,1)} %param.13) | copy-start | bytes 786436
  7.2 22.1 %copy-start.8 = (s32[1,512]{1,0:T(1,128)S(1)}, s32[1,512]{1,0:T(1,128)}, u32[]{:S(2)}) copy-start(s32[1,512]{1,0:T(1,128)} %param.17) | copy-start | bytes 6148
  7.2 23.3 %copy-start.4 = (bf16[512,512]{1,0:T(8,128)(2,1)S(1)}, bf16[512,512]{1,0:T(8,128)(2,1)}, u32[]{:S(2)}) copy-start(bf16[512,512]{1,0:T(8,128)(2,1)} %param.20) | copy-start | bytes 1572868
  8.7 23.8 %all-to-all-start = ((bf16[16,1,16]{2,1,0:T(2,128)(2,1)}), bf16[16,1,16]{2,1,0:T(2,128)(2,1)S(1)}, u32[]{:S(2)}, u32[]{:S(2)}) async-start(bf16[16,1,16]{2,1,0:T(2,128)(2,1)} %compare_convert_fusion), calls=%async_computation | async-start | bytes 16384 | tf_op jit(solution)/shard_map/all_to_all | solution.py:73
  16.1 87.5 %reduce-scatter.3.cloned.1.call-start = ((), (), s32[]{:S(2)}) async-start(), calls=%async_computation.3 | async-start | bytes 98304 | tf_op jit(solution)/shard_map/reduce_scatter | solution.py:104
  20.1 60.1 %collective-permute-start.14 = (bf16[1,16,512]{2,1,0:T(8,128)(2,1)S(1)}, bf16[1,16,512]{2,1,0:T(8,128)(2,1)}, u32[]{:S(2)}, u32[]{:S(2)}) collective-permute-start(bf16[1,16,512]{2,1,0:T(8,128)(2,1)S(1)} %get-tuple-element.2), channel_id=1, source_target_pairs={{0,15},{1,14},{2,13},{3,12},{4,11},{5,10},{6,9},{7,8},{8,7},{9,6},... | collective-permute-start | bytes 49160 | tf_op jit(solution)/shard_map/ppermute | solution.py:26
  24.4 55.1 %collective-permute-start.13 = (bf16[1,16,512]{2,1,0:T(8,128)(2,1)S(1)}, bf16[1,16,512]{2,1,0:T(8,128)(2,1)}, u32[]{:S(2)}, u32[]{:S(2)}) collective-permute-start(bf16[1,16,512]{2,1,0:T(8,128)(2,1)S(1)} %get-tuple-element.3), channel_id=1, source_target_pairs={{0,14},{1,15},{2,12},{3,13},{4,10},{5,11},{6,8},{7,9},{8,6},{9,7},... | collective-permute-start | bytes 49160 | tf_op jit(solution)/shard_map/ppermute | solution.py:26
  24.8 54.0 %collective-permute-start.12 = (bf16[1,16,512]{2,1,0:T(8,128)(2,1)S(1)}, bf16[1,16,512]{2,1,0:T(8,128)(2,1)}, u32[]{:S(2)}, u32[]{:S(2)}) collective-permute-start(bf16[1,16,512]{2,1,0:T(8,128)(2,1)S(1)} %get-tuple-element.4), channel_id=1, source_target_pairs={{0,13},{1,12},{2,15},{3,14},{4,9},{5,8},{6,11},{7,10},{8,5},{9,4},... | collective-permute-start | bytes 49160 | tf_op jit(solution)/shard_map/ppermute | solution.py:26
  27.9 50.1 %collective-permute-start.11 = (bf16[1,16,512]{2,1,0:T(8,128)(2,1)S(1)}, bf16[1,16,512]{2,1,0:T(8,128)(2,1)}, u32[]{:S(2)}, u32[]{:S(2)}) collective-permute-start(bf16[1,16,512]{2,1,0:T(8,128)(2,1)S(1)} %get-tuple-element.5), channel_id=1, source_target_pairs={{0,12},{1,13},{2,14},{3,15},{4,8},{5,9},{6,10},{7,11},{8,4},{9,5},... | collective-permute-start | bytes 49160 | tf_op jit(solution)/shard_map/ppermute | solution.py:26
  28.2 6.7 %collective-permute-start = (bf16[1,16,512]{2,1,0:T(8,128)(2,1)}, bf16[1,16,512]{2,1,0:T(8,128)(2,1)}, u32[]{:S(2)}, u32[]{:S(2)}) collective-permute-start(bf16[1,16,512]{2,1,0:T(8,128)(2,1)} %get-tuple-element.16), channel_id=1, source_target_pairs={{0,1},{1,0},{2,3},{3,2},{4,5},{5,4},{6,7},{7,6},{8,9},{9,8},{10,11... | collective-permute-start | bytes 49160 | tf_op jit(solution)/shard_map/ppermute | solution.py:26
  35.0 4.0 %collective-permute-start.1 = (bf16[1,16,512]{2,1,0:T(8,128)(2,1)}, bf16[1,16,512]{2,1,0:T(8,128)(2,1)S(1)}, u32[]{:S(2)}, u32[]{:S(2)}) collective-permute-start(bf16[1,16,512]{2,1,0:T(8,128)(2,1)} %get-tuple-element.15), channel_id=1, source_target_pairs={{0,2},{1,3},{2,0},{3,1},{4,6},{5,7},{6,4},{7,5},{8,10},{9,11},{10,... | collective-permute-start | bytes 49160 | tf_op jit(solution)/shard_map/ppermute | solution.py:26
  39.0 3.4 %collective-permute-start.2 = (bf16[1,16,512]{2,1,0:T(8,128)(2,1)}, bf16[1,16,512]{2,1,0:T(8,128)(2,1)S(1)}, u32[]{:S(2)}, u32[]{:S(2)}) collective-permute-start(bf16[1,16,512]{2,1,0:T(8,128)(2,1)} %get-tuple-element.14), channel_id=1, source_target_pairs={{0,3},{1,2},{2,1},{3,0},{4,7},{5,6},{6,5},{7,4},{8,11},{9,10},{10,... | collective-permute-start | bytes 49160 | tf_op jit(solution)/shard_map/ppermute | solution.py:26
  42.4 3.9 %collective-permute-start.3 = (bf16[1,16,512]{2,1,0:T(8,128)(2,1)}, bf16[1,16,512]{2,1,0:T(8,128)(2,1)S(1)}, u32[]{:S(2)}, u32[]{:S(2)}) collective-permute-start(bf16[1,16,512]{2,1,0:T(8,128)(2,1)} %get-tuple-element.13), channel_id=1, source_target_pairs={{0,4},{1,5},{2,6},{3,7},{4,0},{5,1},{6,2},{7,3},{8,12},{9,13},{10,... | collective-permute-start | bytes 49160 | tf_op jit(solution)/shard_map/ppermute | solution.py:26
  46.3 3.4 %collective-permute-start.4 = (bf16[1,16,512]{2,1,0:T(8,128)(2,1)}, bf16[1,16,512]{2,1,0:T(8,128)(2,1)S(1)}, u32[]{:S(2)}, u32[]{:S(2)}) collective-permute-start(bf16[1,16,512]{2,1,0:T(8,128)(2,1)} %get-tuple-element.12), channel_id=1, source_target_pairs={{0,5},{1,4},{2,7},{3,6},{4,1},{5,0},{6,3},{7,2},{8,13},{9,12},{10,... | collective-permute-start | bytes 49160 | tf_op jit(solution)/shard_map/ppermute | solution.py:26
  49.7 4.8 %collective-permute-start.5 = (bf16[1,16,512]{2,1,0:T(8,128)(2,1)}, bf16[1,16,512]{2,1,0:T(8,128)(2,1)S(1)}, u32[]{:S(2)}, u32[]{:S(2)}) collective-permute-start(bf16[1,16,512]{2,1,0:T(8,128)(2,1)} %get-tuple-element.11), channel_id=1, source_target_pairs={{0,6},{1,7},{2,4},{3,5},{4,2},{5,3},{6,0},{7,1},{8,14},{9,15},{10,... | collective-permute-start | bytes 49160 | tf_op jit(solution)/shard_map/ppermute | solution.py:26
  54.5 4.3 %collective-permute-start.6 = (bf16[1,16,512]{2,1,0:T(8,128)(2,1)}, bf16[1,16,512]{2,1,0:T(8,128)(2,1)S(1)}, u32[]{:S(2)}, u32[]{:S(2)}) collective-permute-start(bf16[1,16,512]{2,1,0:T(8,128)(2,1)} %get-tuple-element.10), channel_id=1, source_target_pairs={{0,7},{1,6},{2,5},{3,4},{4,3},{5,2},{6,1},{7,0},{8,15},{9,14},{10,... | collective-permute-start | bytes 49160 | tf_op jit(solution)/shard_map/ppermute | solution.py:26
  58.8 4.6 %collective-permute-start.7 = (bf16[1,16,512]{2,1,0:T(8,128)(2,1)S(1)}, bf16[1,16,512]{2,1,0:T(8,128)(2,1)S(1)}, u32[]{:S(2)}, u32[]{:S(2)}) collective-permute-start(bf16[1,16,512]{2,1,0:T(8,128)(2,1)S(1)} %get-tuple-element.9), channel_id=1, source_target_pairs={{0,8},{1,9},{2,10},{3,11},{4,12},{5,13},{6,14},{7,15},{8,0},{9,1},... | collective-permute-start | bytes 49160 | tf_op jit(solution)/shard_map/ppermute | solution.py:26
  63.4 4.1 %collective-permute-start.8 = (bf16[1,16,512]{2,1,0:T(8,128)(2,1)S(1)}, bf16[1,16,512]{2,1,0:T(8,128)(2,1)S(1)}, u32[]{:S(2)}, u32[]{:S(2)}) collective-permute-start(bf16[1,16,512]{2,1,0:T(8,128)(2,1)S(1)} %get-tuple-element.8), channel_id=1, source_target_pairs={{0,9},{1,8},{2,11},{3,10},{4,13},{5,12},{6,15},{7,14},{8,1},{9,0},... | collective-permute-start | bytes 49160 | tf_op jit(solution)/shard_map/ppermute | solution.py:26
  67.5 5.5 %collective-permute-start.9 = (bf16[1,16,512]{2,1,0:T(8,128)(2,1)S(1)}, bf16[1,16,512]{2,1,0:T(8,128)(2,1)S(1)}, u32[]{:S(2)}, u32[]{:S(2)}) collective-permute-start(bf16[1,16,512]{2,1,0:T(8,128)(2,1)S(1)} %get-tuple-element.7), channel_id=1, source_target_pairs={{0,10},{1,11},{2,8},{3,9},{4,14},{5,15},{6,12},{7,13},{8,2},{9,3},... | collective-permute-start | bytes 49160 | tf_op jit(solution)/shard_map/ppermute | solution.py:26
  73.1 5.0 %collective-permute-start.10 = (bf16[1,16,512]{2,1,0:T(8,128)(2,1)S(1)}, bf16[1,16,512]{2,1,0:T(8,128)(2,1)S(1)}, u32[]{:S(2)}, u32[]{:S(2)}) collective-permute-start(bf16[1,16,512]{2,1,0:T(8,128)(2,1)S(1)} %get-tuple-element.6), channel_id=1, source_target_pairs={{0,11},{1,10},{2,9},{3,8},{4,15},{5,14},{6,13},{7,12},{8,3},{9,2},... | collective-permute-start | bytes 49160 | tf_op jit(solution)/shard_map/ppermute | solution.py:26
  92.4 76.7 %reduce-scatter.5.cloned.1.call-start = ((), (), s32[]{:S(2)}) async-start(), calls=%async_computation.4 | async-start | bytes 2228224 | tf_op jit(solution)/shard_map/reduce_scatter | solution.py:116
  106.9 84.9 %all-reduce.2.cloned.1.call-start = ((), (), s32[]{:S(2)}) async-start(), calls=%async_computation.5 | async-start | bytes 131072 | tf_op jit(solution)/shard_map/psum | solution.py:119
  (7 other events, 80.6 us)
Sparse Core Ops, SparseCore 0:
  92.5 11.0 reduce-scatter.2
  107.3 61.7 reduce-scatter.4
  172.0 19.8 all-reduce.1
